TPU v7x, 128 devices: a whole 4x4x4 slice. The times are simulated.
128 devices in a mesh: gx: 16 (over z, x_hi, core), gy: 8 (over x_lo, y).
Axes of the slice: x: 4 (x_hi: 2, x_lo: 2; x = x_hi * 2 + x_lo), y: 4, z: 4, core: 2. Of those that a mesh axis runs over, the one named last changes fastest.
Arguments:
- grid_field: bfloat16 [1, 20, 2048, 2048], P(None, None, 'gx', 'gy'), may hold values from -8 to 8
- spectral_weight: float32 [2, 2, 20, 20, 2048], P(None, None, None, None, ('gx', 'gy')), may hold values from -1 to 1
- conv_near: bfloat16 [2, 20, 180], replicated, may hold values from -0.4375 to 0.4375
- conv_far: bfloat16 [2, 20, 500], replicated, may hold values from -0.25 to 0.25
- mix_logits: float32 [2, 3], replicated, may hold values from -1 to 1
- channel_bias: float32 [2, 20], replicated, may hold values from -3 to 3
Outputs:
- result_field: bfloat16 [1, 20, 2048, 2048], P(None, None, 'gx', 'gy')
All inputs are finite; a program needn't handle non-finite values.
Results may differ from a plain program's by a relative error of at most 0.004.
Values may be sent and summed in bfloat16 or wider, within the bound.
No kernel may reach another device: no remote copies, remote signals or barrier semaphores. Data moves between devices by JAX's collectives and lax.ppermute only.
A program may use at most 192 MiB of HBM per device.

v0:
```python
import math
import jax
import jax.numpy as jnp
from jax import lax
from jax.sharding import PartitionSpec as P

NX = 2048
NY = 2048
MX = 32
MY = 32
LAYERS = 2
KX = 64
MODES = 2048
full_turn = 2.0 * math.pi
highest = lax.Precision.HIGHEST


def padded_2(value, sides, width):
    for axis, dim in sides:
        size, length = (lax.axis_size(axis), value.shape[dim])
        up = [(i, (i + 1) % size) for i in range(size)]
        down = [(j, i) for i, j in up]
        last = lax.slice_in_dim(value, length - width, length, axis=dim)
        first = lax.slice_in_dim(value, 0, width, axis=dim)
        before = lax.ppermute(last, axis, up)
        after = lax.ppermute(first, axis, down)
        value = jnp.concatenate([before, value, after], axis=dim)
    return value


def forward_table(positions):
    col_modes = jnp.arange(MY, dtype=jnp.int32)
    phases = (positions[:, None] * col_modes[None, :] % NY).astype(jnp.float32) * (full_turn / NY)
    return jnp.concatenate([jnp.cos(phases), -jnp.sin(phases)], axis=1).astype(jnp.bfloat16)


def row_tables(positions):
    lower = jnp.arange(MX, dtype=jnp.int32)
    row_modes = jnp.concatenate([lower, lower + (NX - MX)])
    phases = (positions[:, None] * row_modes[None, :] % NX).astype(jnp.float32) * (full_turn / NX)
    return (jnp.cos(phases), jnp.sin(phases))


def inverse_table(positions):
    col_modes = jnp.arange(MY, dtype=jnp.int32)
    col_weight = jnp.where(col_modes == 0, 1.0, 2.0).astype(jnp.float32) / (NX * NY)
    phases = (col_modes[:, None] * positions[None, :] % NY).astype(jnp.float32) * (full_turn / NY)
    return jnp.concatenate(
        [jnp.cos(phases) * col_weight[:, None], -jnp.sin(phases) * col_weight[:, None]], axis=0
    )


def conv_rows(padded_plane, tap_weights, dilation, side_taps, first_row, count_rows, local_cols):
    channels = padded_plane.shape[0]
    pieces = []
    for row_tap in range(side_taps):
        for col_tap in range(side_taps):
            row_offset = 4 + (row_tap - side_taps // 2) * dilation + first_row
            col_offset = 4 + (col_tap - side_taps // 2) * dilation
            pieces.append(
                padded_plane[
                    :, row_offset : row_offset + count_rows, col_offset : col_offset + local_cols
                ]
            )
    stacked = jnp.stack(pieces, 0)
    shaped_weights = tap_weights.reshape(channels, side_taps * side_taps, channels)
    return jnp.einsum("otc,tcxy->oxy", shaped_weights, stacked, preferred_element_type=jnp.float32)


def on_device(grid_field, spectral_weight, conv_near, conv_far, mix_logits, channel_bias):
    channels = grid_field.shape[1]
    local_rows = grid_field.shape[2]
    local_cols = grid_field.shape[3]
    row_positions = lax.axis_index("gx") * local_rows + jnp.arange(local_rows, dtype=jnp.int32)
    col_positions = lax.axis_index("gy") * local_cols + jnp.arange(local_cols, dtype=jnp.int32)
    forward_cols = forward_table(col_positions)
    cosine_rows, sine_rows = row_tables(row_positions)
    inverse_cols = inverse_table(col_positions)
    share_modes = spectral_weight.shape[-1]
    owner_index = lax.axis_index("gx") * lax.axis_size("gy") + lax.axis_index("gy")
    mode_start = owner_index * share_modes
    row_blocks = max(1, local_rows // 32)
    while local_rows % row_blocks != 0:
        row_blocks = row_blocks - 1
    block_rows = local_rows // row_blocks
    planes_block = grid_field
    for layer_index in range(LAYERS):
        planes_here = planes_block.shape[0]
        line_sums = jnp.dot(
            planes_block.reshape(planes_here * channels * local_rows, local_cols),
            forward_cols,
            preferred_element_type=jnp.float32,
        )
        line_sums = line_sums.reshape(planes_here, channels, local_rows, 2 * MY)
        real_lines = line_sums[..., :MY]
        imaginary_lines = line_sums[..., MY:]

        def contract_rows(operand, lookup):
            return jnp.einsum("pcxk,xj->pcjk", operand, lookup, precision=highest)

        real_spec = contract_rows(real_lines, cosine_rows) + contract_rows(
            imaginary_lines, sine_rows
        )
        imaginary_spec = contract_rows(imaginary_lines, cosine_rows) - contract_rows(
            real_lines, sine_rows
        )
        partial_value = jnp.stack(
            [
                real_spec.reshape(planes_here, channels, MODES),
                imaginary_spec.reshape(planes_here, channels, MODES),
            ]
        )
        totals = lax.psum(partial_value, ("gx", "gy"))
        own_modes = lax.dynamic_slice_in_dim(totals, mode_start, share_modes, 3)

        def mix_modes(spectrum, weights):
            return jnp.einsum("pcm,com->pom", spectrum, weights, precision=highest)

        weight_real = spectral_weight[layer_index, 0]
        weight_imaginary = spectral_weight[layer_index, 1]
        real_mixed = mix_modes(own_modes[0], weight_real) - mix_modes(
            own_modes[1], weight_imaginary
        )
        imaginary_mixed = mix_modes(own_modes[1], weight_real) + mix_modes(
            own_modes[0], weight_imaginary
        )
        own_block = jnp.stack([real_mixed, imaginary_mixed])[None]
        gathered = lax.all_gather(own_block, ("gx", "gy"), axis=0, tiled=True)
        gathered = jnp.transpose(gathered, (1, 2, 3, 0, 4)).reshape(2, planes_here, channels, MODES)
        real_full = gathered[0].reshape(planes_here, channels, KX, MY)
        imaginary_full = gathered[1].reshape(planes_here, channels, KX, MY)

        def expand_rows(spectrum, lookup):
            return jnp.einsum("pcjk,xj->pcxk", spectrum, lookup, precision=highest)

        real_rows = expand_rows(real_full, cosine_rows) - expand_rows(imaginary_full, sine_rows)
        imaginary_rows = expand_rows(real_full, sine_rows) + expand_rows(
            imaginary_full, cosine_rows
        )
        stacked = jnp.concatenate([real_rows, imaginary_rows], axis=-1).reshape(
            planes_here * channels * local_rows, 2 * MY
        )
        spectral = jnp.dot(stacked, inverse_cols, precision=highest)
        layer_spectral = spectral.reshape(planes_here, channels, local_rows, local_cols)
        padded = padded_2(planes_block, (("gx", 2), ("gy", 3)), 4)
        exponents = jnp.exp(mix_logits[layer_index])
        mixture = exponents / jnp.sum(exponents)
        bias_column = channel_bias[layer_index][:, None, None]
        row_pieces = []
        for block_index in range(row_blocks):
            first_row = block_index * block_rows
            near_term = conv_rows(
                padded[0], conv_near[layer_index], 1, 3, first_row, block_rows, local_cols
            )
            far_term = conv_rows(
                padded[0], conv_far[layer_index], 2, 5, first_row, block_rows, local_cols
            )
            spectral_rows = layer_spectral[0, :, first_row : first_row + block_rows, :]
            summed = (
                mixture[0] * spectral_rows
                + mixture[1] * near_term
                + mixture[2] * far_term
                + bias_column
            )
            row_pieces.append(jax.nn.gelu(summed, approximate=False).astype(jnp.bfloat16))
        outputs = [jnp.concatenate(row_pieces, axis=1)]
        planes_block = jnp.stack(outputs)
    return planes_block


def solution(mesh):
    in_specs = (
        P(None, None, "gx", "gy"),
        P(None, None, None, None, ("gx", "gy")),
        P(),
        P(),
        P(),
        P(),
    )
    out_specs = P(None, None, "gx", "gy")
    return jax.shard_map(
        on_device, mesh=mesh, in_specs=in_specs, out_specs=out_specs, check_vma=False
    )
```

profile of v0, /device:TPU:0, one launch (start us, length us, event | category | flops | bytes accessed | tf_op | source)
XLA Modules:
  0.0 1025.7 jit_solution(15079216024907753427)
XLA Ops:
  8.8 6.0 collective-permute-start.1
  15.0 1.9 convolution_bitcast_fusion
  23.0 2.0 slice_bitcast_fusion.263
  27.7 2.0 broadcast_divide_fusion.1
  29.7 1.5 slice_reduce_fusion.2
  35.1 1.6 collective-permute-start.2
  37.3 2.9 collective-permute-start.3
  40.8 1.7 reshape_squeeze.9
  42.5 1.5 reshape_squeeze.8
  45.9 1.4 reshape_squeeze.10
  49.2 1.6 maximum_bitcast_fusion
  58.5 1.5 constant_dynamic-update-slice_fusion.29
  60.0 1.5 constant_dynamic-update-slice_fusion.28
  61.5 1.5 constant_dynamic-update-slice_fusion.27
  65.3 1.5 constant_dynamic-update-slice_fusion.24
  67.1 1.5 constant_dynamic-update-slice_fusion.23
  68.6 1.5 constant_dynamic-update-slice_fusion.22
  71.0 3.8 copy-done.15
  74.8 14.7 %constant_dynamic-update-slice_fusion.20 = (bf16[25,20,32,256]{3,1,2,0:T(8,128)(2,1)}, bf16[25,20,32,256]{3,1,2,0:T(8,128)(2,1)S(1)}, bf16[9,20,32,256]{3,1,2,0:...) fusion(bf16[25,20,32,256]{3,1,2,0:T(8,128)(2,1)} %get-tuple-ele, ...), kind=kLoop, calls=%fused_computation.275 | loop fusion | bytes 5505024
  89.7 1.9 constant_dynamic-update-slice_fusion.19
  91.6 1.9 constant_dynamic-update-slice_fusion.18
  93.4 1.7 constant_dynamic-update-slice_fusion.17
  95.2 1.5 constant_dynamic-update-slice_fusion.16
  96.6 1.9 constant_dynamic-update-slice_fusion.15
  98.5 1.8 constant_dynamic-update-slice_fusion.14
  100.3 1.8 constant_dynamic-update-slice_fusion.13
  102.1 1.7 constant_dynamic-update-slice_fusion.12
  104.6 2.3 convolution_bitcast_fusion.3
  106.9 2.4 convolution_bitcast_fusion.5
  109.3 6.5 convolution_bitcast_fusion.7
  115.8 2.3 convolution_bitcast_fusion.9
  118.8 1.5 convolution_bitcast_fusion.6
  120.4 1.5 convolution_bitcast_fusion.8
  123.3 1.5 convolution_bitcast_fusion.10
  124.9 39.9 %all-reduce.3.cloned.1.call-done = f32[2,1,20,2048]{3,0,2,1:T(2,128)} async-done(((f32[2,1,20,2048]{3,0,2,1:T(2,128)}), f32[2,1,20,2048]{3,0,2,1:T(2,128)}) %all-reduce.3.cloned.1.call-update) | async-done | bytes 327696 | tf_op jit(solution)/shard_map/psum | solution.py:113
  167.1 326.2 %all-gather = f32[256,1,20,16]{2,3,1,0:T(8,128)S(1)} all-gather(f32[2,1,20,16]{2,3,1,0:T(8,128)S(1)} %pad_maximum_fusion.8), channel_id=2, replica_groups=mesh['gx'=16,'gy'=8] {'gx','gy'}, dimensions={0}, use_global_device_ids=true | all-gather | bytes 330240 | tf_op jit(solution)/shard_map/all_gather | solution.py:128
  500.9 2.2 convolution_bitcast_fusion.2
  503.2 10.4 %fusion.42 = (bf16[20,32,256]{2,1,0:T(8,128)(2,1)S(1)}, bf16[20,32,256]{2,1,0:T(8,128)(2,1)S(1)}, bf16[20,32,256]{2,1,0:T(8,128)(2,1)S(1)}, bf16[20,32,256]{2,1,0:T(8,128)(2,1)S(1)}) fusion(f32[32,256,20]{1,2,0:T(8,128)} %convolution_bitcast_fusion.9, f32[32,256,20]{1,2,0:T(8,128)} %convolution_bitcast_fusion.10, ...), kind=kLoop, calls=%fused_computation.51 | loop fusion | flops 46530560 | bytes 9175132 | tf_op jit(solution)/shard_map/convert_element_type | solution.py:165
  516.9 5.3 collective-permute-start.5
  526.1 4.3 collective-permute-start.7
  532.6 1.8 maximum_bitcast_fusion.1
  548.7 3.2 copy-done.18
  552.0 2.1 constant_dynamic-update-slice_fusion.147
  554.4 2.9 constant_dynamic-update-slice_fusion.146
  557.2 2.7 constant_dynamic-update-slice_fusion.145
  560.0 2.6 constant_dynamic-update-slice_fusion.144
  562.6 2.9 constant_dynamic-update-slice_fusion.143
  565.5 2.6 constant_dynamic-update-slice_fusion.142
  568.1 2.6 constant_dynamic-update-slice_fusion.141
  570.7 2.6 constant_dynamic-update-slice_fusion.140
  573.2 2.5 constant_dynamic-update-slice_fusion.139
  576.2 2.8 copy-done.16
  579.2 4.5 fusion.25
  583.7 9.6 fusion.19
  593.3 5.3 fusion.22
  598.6 5.3 fusion.16
  603.8 2.6 fusion.28
  606.4 2.8 fusion.31
  609.2 2.6 fusion.34
  611.7 2.6 fusion.37
  614.3 58.0 %all-reduce.5.cloned.1.call-done = f32[2,1,20,2048]{3,0,2,1:T(2,128)} async-done(((f32[2,1,20,2048]{3,0,2,1:T(2,128)}), f32[2,1,20,2048]{3,0,2,1:T(2,128)}) %all-reduce.5.cloned.1.call-update) | async-done | bytes 327696 | tf_op jit(solution)/shard_map/psum | solution.py:113
  674.7 325.8 %all-gather.1 = f32[256,1,20,16]{2,3,1,0:T(8,128)S(1)} all-gather(f32[2,1,20,16]{2,3,1,0:T(8,128)S(1)} %pad_maximum_fusion.9), channel_id=3, replica_groups=mesh['gx'=16,'gy'=8] {'gx','gy'}, dimensions={0}, use_global_device_ids=true | all-gather | bytes 330240 | tf_op jit(solution)/shard_map/all_gather | solution.py:128
  1004.6 2.2 convolution_bitcast_fusion.1
  1006.8 10.5 %fusion.54 = (bf16[20,32,256]{2,1,0:T(8,128)(2,1)S(1)}, bf16[20,32,256]{2,1,0:T(8,128)(2,1)S(1)}, bf16[20,32,256]{2,1,0:T(8,128)(2,1)S(1)}, bf16[20,32,256]{2,1,0:T(8,128)(2,1)S(1)}) fusion(f32[32,256,20]{1,2,0:T(8,128)} %fusion.16, f32[32,256,20]{1,2,0:T(8,128)} %fusion.28, f32[1,20,128,256]{3,2,1,0:T(8,128)S(1)} %convolution_bitcast_fusion.1, ...), kind=kLoop, calls=%fused_computation.63 | loop fusion | flops 46530560 | bytes 9175132 | tf_op jit(solution)/shard_map/convert_element_type | solution.py:165
  (209 shorter events, 75.8 us)
Async XLA Ops:
  6.5 15.6 %copy-start.8 = (bf16[2,20,500]{2,0,1:T(2,128)(2,1)S(1)}, bf16[2,20,500]{2,0,1:T(2,128)(2,1)}, u32[]{:S(2)}) copy-start(bf16[2,20,500]{2,0,1:T(2,128)(2,1)} %param.9) | copy-start | bytes 120004
  6.5 158.2 %all-reduce.3.cloned.1.call-start = ((), (), s32[]{:S(2)}) async-start(), calls=%async_computation | async-start | bytes 655360 | tf_op jit(solution)/shard_map/psum | solution.py:113
  8.1 23.0 %collective-permute-start = (bf16[1,20,4,256]{3,1,2,0:T(8,128)(2,1)}, bf16[1,20,4,256]{3,1,2,0:T(8,128)(2,1)}, u32[]{:S(2)}, u32[]{:S(2)}) collective-permute-start(bf16[1,20,4,256]{3,1,2,0:T(8,128)(2,1)} %copy.500), channel_id=1, source_target_pairs={{0,8},{8,16},{16,24},{24,32},{32,40},{40,48},{48,56},{56,64},{64,7... | collective-permute-start | bytes 122888 | tf_op jit(solution)/shard_map/ppermute | solution.py:25
  8.8 24.0 %collective-permute-start.1 = (bf16[1,20,4,256]{3,1,2,0:T(8,128)(2,1)}, bf16[1,20,4,256]{3,1,2,0:T(8,128)(2,1)}, u32[]{:S(2)}, u32[]{:S(2)}) collective-permute-start(bf16[1,20,4,256]{3,1,2,0:T(8,128)(2,1)} %copy.501), channel_id=1, source_target_pairs={{8,0},{16,8},{24,16},{32,24},{40,32},{48,40},{56,48},{64,56},{72,6... | collective-permute-start | bytes 122888 | tf_op jit(solution)/shard_map/ppermute | solution.py:26
  15.0 7.2 copy-start.11
  15.0 7.2 copy-start.13
  15.0 10.7 %copy-start.19 = (f32[2,3]{1,0:T(2,128)S(1)}, f32[2,3]{1,0:T(2,128)}, u32[]{:S(2)}) copy-start(f32[2,3]{1,0:T(2,128)} %param.10) | copy-start | bytes 76
  15.0 17.0 %copy-start = (bf16[1,20,128,256]{3,2,1,0:T(8,128)(2,1)S(1)}, bf16[1,20,128,256]{3,2,1,0:T(8,128)(2,1)}, u32[]{:S(2)}) copy-start(bf16[1,20,128,256]{3,2,1,0:T(8,128)(2,1)} %param.6) | copy-start | bytes 3932164
  22.1 650.2 %all-reduce.5.cloned.1.call-start = ((), (), s32[]{:S(2)}) async-start(), calls=%async_computation.1 | async-start | bytes 655360 | tf_op jit(solution)/shard_map/psum | solution.py:113
  35.1 12.2 %collective-permute-start.2 = (bf16[1,20,136,4]{2,3,1,0:T(4,128)(2,1)}, bf16[1,20,136,4]{2,3,1,0:T(4,128)(2,1)S(1)}, u32[]{:S(2)}, u32[]{:S(2)}) collective-permute-start(bf16[1,20,136,4]{2,3,1,0:T(4,128)(2,1)} %copy.211), channel_id=1, source_target_pairs={{0,1},{1,2},{2,3},{3,4},{4,5},{5,6},{6,7},{7,0},{8,9},{9,10},{10,1... | collective-permute-start | bytes 65288 | tf_op jit(solution)/shard_map/ppermute | solution.py:25
  37.3 10.6 %collective-permute-start.3 = (bf16[1,20,136,4]{2,3,1,0:T(4,128)(2,1)S(1)}, bf16[1,20,136,4]{2,3,1,0:T(4,128)(2,1)}, u32[]{:S(2)}, u32[]{:S(2)}) collective-permute-start(bf16[1,20,136,4]{2,3,1,0:T(4,128)(2,1)S(1)} %copy.212), channel_id=1, source_target_pairs={{1,0},{2,1},{3,2},{4,3},{5,4},{6,5},{7,6},{0,7},{9,8},{10,9},{11,1... | collective-permute-start | bytes 65288 | tf_op jit(solution)/shard_map/ppermute | solution.py:26
  71.0 3.8 copy-start.15
  100.3 4.3 copy-start.7
  106.9 8.9 slice-start
  106.9 8.9 slice-start.1
  109.3 6.5 slice-start.2
  115.8 2.4 copy-start.5
  120.4 45.4 %copy-start.4 = (f32[20,20,16]{1,2,0:T(8,128)S(1)}, f32[20,20,16]{1,2,0:T(8,128)}, u32[]{:S(2)}) copy-start(f32[20,20,16]{1,2,0:T(8,128)} %get-tuple-element.287) | copy-start | bytes 76804
  120.4 46.1 %copy-start.3 = (f32[20,20,16]{1,2,0:T(8,128)S(1)}, f32[20,20,16]{1,2,0:T(8,128)}, u32[]{:S(2)}) copy-start(f32[20,20,16]{1,2,0:T(8,128)} %get-tuple-element.286) | copy-start | bytes 76804
  124.9 376.1 %copy-start.6 = (f32[32,256]{1,0:T(8,128)S(1)}, f32[32,256]{1,0:T(8,128)}, u32[]{:S(2)}) copy-start(f32[32,256]{1,0:T(8,128)} %get-tuple-element.296) | copy-start | bytes 98308
  167.1 336.1 %copy-start.21 = (f32[20]{0:T(128)S(1)}, f32[20]{0:T(128)}, u32[]{:S(2)}) copy-start(f32[20]{0:T(128)} %get-tuple-element.300) | copy-start | bytes 244
  494.2 9.0 copy-start.1
  500.9 12.8 %copy-start.12 = (bf16[256,32]{0,1:T(8,128)(2,1)S(1)}, bf16[256,32]{0,1:T(8,128)(2,1)}, u32[]{:S(2)}) copy-start(bf16[256,32]{0,1:T(8,128)(2,1)} %copy-done.11) | copy-start | bytes 49156
  500.9 12.8 %copy-start.14 = (bf16[256,32]{0,1:T(8,128)(2,1)S(1)}, bf16[256,32]{0,1:T(8,128)(2,1)}, u32[]{:S(2)}) copy-start(bf16[256,32]{0,1:T(8,128)(2,1)} %copy-done.13) | copy-start | bytes 49156
  516.8 7.1 collective-permute-start.4
  516.9 7.0 collective-permute-start.5
  525.6 6.2 collective-permute-start.6
  526.1 6.0 collective-permute-start.7
  548.7 3.2 copy-start.18
  568.1 11.1 %copy-start.9 = (bf16[20,25,20]{1,0,2:T(8,128)(2,1)S(1)}, bf16[20,25,20]{1,0,2:T(8,128)(2,1)}, u32[]{:S(2)}) copy-start(bf16[20,25,20]{1,0,2:T(8,128)(2,1)} %copy.257) | copy-start | bytes 60004
  575.7 3.3 copy-start.16
  583.7 9.6 copy-start.17
  598.6 5.3 copy-start.10
  606.4 66.9 %copy-start.2 = (f32[20,20,16]{1,2,0:T(8,128)S(1)}, f32[20,20,16]{1,2,0:T(8,128)}, u32[]{:S(2)}) copy-start(f32[20,20,16]{1,2,0:T(8,128)} %get-tuple-element.285) | copy-start | bytes 76804
  674.7 332.2 %copy-start.20 = (f32[20]{0:T(128)S(1)}, f32[20]{0:T(128)}, u32[]{:S(2)}) copy-start(f32[20]{0:T(128)} %get-tuple-element.299) | copy-start | bytes 244
Sparse Core Ops, SparseCore 0:
  22.2 142.4 all-reduce.2
  531.7 140.5 all-reduce.4
where the time goes:
time: 1030 us
  blocking collectives  652 us (63%)
  local copies, waits for them, and re-layouts  131 us (13%)
  waiting for transfers between devices  98.6 us (10%)
  matrix products  74.6 us (7%)
  other arithmetic  34.5 us (3%)
  starting transfers between devices  20.3 us (2%)
  between operations  14.7 us (1%)
    all_gather x2, blocking collectives, on_device(): gathered = lax.all_gather(own_block, ('gx', 'gy'), axis=0, tiled=True)  652 us
    unnamed x121, local copies, waits for them, and re-layouts  98.1 us
    psum x2, waiting for transfers between devices, on_device(): totals = lax.psum(partial_value, ('gx', 'gy'))  97.8 us
    dot_general x16, matrix products, conv_rows(): jnp.einsum('otc,tcxy->oxy', shaped_weights, stacked, preferred_element_ty...  53.9 us
    convert_element_type x2, other arithmetic, on_device(): jax.nn.gelu(summed, approximate=False).astype(jnp.bfloat16)  20.9 us
  transfers between devices with their start and end apart: 10, of which 4 were waited for; matrix products, arithmetic and copies ran while one was open for 18% of the time, Pallas kernels for 0%

commit v1 on v0

--- a/solution.py
+++ b/solution.py
@@ -110,7 +110,7 @@
                 imaginary_spec.reshape(planes_here, channels, MODES),
             ]
         )
-        totals = lax.psum(partial_value, ("gx", "gy"))
+        totals = lax.psum(lax.psum(partial_value, "gx"), "gy")
         own_modes = lax.dynamic_slice_in_dim(totals, mode_start, share_modes, 3)
 
         def mix_modes(spectrum, weights):

time: 1030 us -> 1160 us (1.13)
  waiting for transfers between devices: 98.6 us -> 230 us
    psum x2 -> x4, waiting for transfers between devices: 97.8 us -> 229 us  [on_device(): totals = lax.psum(lax.psum(partial_value, 'gx'), 'gy')]
  transfers between devices with their start and end apart: 10 -> 12, of which waited for: 4 -> 7; matrix products, arithmetic and copies ran while one was open for 18% -> 16% of each run, Pallas kernels for 0% -> 0%
where the time goes in v1:
time: 1160 us
  blocking collectives  643 us (55%)
  waiting for transfers between devices  230 us (20%)
  local copies, waits for them, and re-layouts  131 us (11%)
  matrix products  82.2 us (7%)
  other arithmetic  35.4 us (3%)
  starting transfers between devices  20.5 us (2%)
  between operations  14.4 us (1%)
    all_gather x2, blocking collectives, on_device(): gathered = lax.all_gather(own_block, ('gx', 'gy'), axis=0, tiled=True)  643 us
    psum x4, waiting for transfers between devices, on_device(): totals = lax.psum(lax.psum(partial_value, 'gx'), 'gy')  229 us
    unnamed x121, local copies, waits for them, and re-layouts  105 us
    dot_general x16, matrix products, conv_rows(): jnp.einsum('otc,tcxy->oxy', shaped_weights, stacked, preferred_element_ty...  57.8 us
  transfers between devices with their start and end apart: 12, of which 7 were waited for; matrix products, arithmetic and copies ran while one was open for 16% of the time, Pallas kernels for 0%

profile of v1, /device:TPU:0, one launch (start us, length us, event | category | flops | bytes accessed | tf_op | source)
XLA Modules:
  0.0 1156.6 jit_solution(6715790735440874151)
XLA Ops:
  8.8 6.0 collective-permute-start.1
  15.0 1.9 convolution_bitcast_fusion
  22.4 2.0 slice_bitcast_fusion.263
  30.2 1.6 collective-permute-start.2
  32.4 2.9 collective-permute-start.3
  41.6 3.2 maximum_bitcast_fusion
  53.4 1.5 constant_dynamic-update-slice_fusion.29
  54.9 1.5 constant_dynamic-update-slice_fusion.28
  56.4 1.5 constant_dynamic-update-slice_fusion.27
  60.1 1.5 constant_dynamic-update-slice_fusion.24
  61.9 1.5 constant_dynamic-update-slice_fusion.23
  63.5 1.5 constant_dynamic-update-slice_fusion.22
  65.8 3.8 copy-done.16
  69.6 14.6 %constant_dynamic-update-slice_fusion.20 = (bf16[25,20,32,256]{3,1,2,0:T(8,128)(2,1)}, bf16[25,20,32,256]{3,1,2,0:T(8,128)(2,1)S(1)}, bf16[9,20,32,256]{3,1,2,0:...) fusion(bf16[25,20,32,256]{3,1,2,0:T(8,128)(2,1)} %get-tuple-ele, ...), kind=kLoop, calls=%fused_computation.275 | loop fusion | bytes 5505024
  84.5 1.9 constant_dynamic-update-slice_fusion.19
  86.3 1.9 constant_dynamic-update-slice_fusion.18
  88.2 1.7 constant_dynamic-update-slice_fusion.17
  89.9 1.5 constant_dynamic-update-slice_fusion.16
  91.4 1.9 constant_dynamic-update-slice_fusion.15
  93.3 1.8 constant_dynamic-update-slice_fusion.14
  95.1 1.8 constant_dynamic-update-slice_fusion.13
  96.9 1.7 constant_dynamic-update-slice_fusion.12
  99.3 2.4 convolution_bitcast_fusion.3
  101.7 2.4 convolution_bitcast_fusion.5
  104.2 6.4 convolution_bitcast_fusion.7
  110.6 2.3 convolution_bitcast_fusion.9
  113.6 1.5 convolution_bitcast_fusion.6
  122.0 1.5 convolution_bitcast_fusion.8
  123.5 33.1 %all-reduce.5.cloned.1.call-done = f32[2,1,20,2048]{3,0,2,1:T(2,128)} async-done(((f32[2,1,20,2048]{3,0,2,1:T(2,128)}), f32[2,1,20,2048]{3,0,2,1:T(2,128)}) %all-reduce.5.cloned.1.call-update) | async-done | bytes 327696 | tf_op jit(solution)/shard_map/psum | solution.py:113
  157.6 3.5 convolution_bitcast_fusion.10
  161.2 71.7 %all-reduce.7.cloned.1.call-done = f32[2,1,20,2048]{3,0,2,1:T(2,128)} async-done(((f32[2,1,20,2048]{3,0,2,1:T(2,128)}), f32[2,1,20,2048]{3,0,2,1:T(2,128)}) %all-reduce.7.cloned.1.call-update) | async-done | bytes 327696 | tf_op jit(solution)/shard_map/psum | solution.py:113
  239.0 321.8 %all-gather = f32[256,1,20,16]{2,3,1,0:T(8,128)S(1)} all-gather(f32[2,1,20,16]{2,3,1,0:T(8,128)S(1)} %pad_maximum_fusion.8), channel_id=2, replica_groups=mesh['gx'=16,'gy'=8] {'gx','gy'}, dimensions={0}, use_global_device_ids=true | all-gather | bytes 330240 | tf_op jit(solution)/shard_map/all_gather | solution.py:128
  568.4 2.2 convolution_bitcast_fusion.2
  570.6 10.3 fusion.42
  584.2 5.3 collective-permute-start.5
  592.9 2.2 collective-permute-start.6
  595.6 2.0 collective-permute-start.7
  600.1 1.8 maximum_bitcast_fusion.1
  610.1 1.4 constant_dynamic-update-slice_fusion.161
  614.1 1.4 constant_dynamic-update-slice_fusion.158
  616.2 3.2 copy-done.19
  619.5 2.1 constant_dynamic-update-slice_fusion.147
  621.9 2.9 constant_dynamic-update-slice_fusion.146
  624.7 2.7 constant_dynamic-update-slice_fusion.145
  627.5 2.6 constant_dynamic-update-slice_fusion.144
  630.1 2.9 constant_dynamic-update-slice_fusion.143
  633.0 2.6 constant_dynamic-update-slice_fusion.142
  635.6 2.6 constant_dynamic-update-slice_fusion.141
  638.2 2.6 constant_dynamic-update-slice_fusion.140
  640.7 2.5 constant_dynamic-update-slice_fusion.139
  643.7 2.8 copy-done.17
  646.7 4.5 fusion.25
  651.2 9.6 fusion.19
  660.8 5.3 fusion.22
  666.1 5.3 fusion.16
  671.4 2.6 fusion.28
  673.9 2.8 fusion.31
  676.7 2.6 fusion.34
  679.3 52.4 %all-reduce.9.cloned.1.call-done = f32[2,1,20,2048]{3,0,2,1:T(2,128)} async-done(((f32[2,1,20,2048]{3,0,2,1:T(2,128)}), f32[2,1,20,2048]{3,0,2,1:T(2,128)}) %all-reduce.9.cloned.1.call-update) | async-done | bytes 327696 | tf_op jit(solution)/shard_map/psum | solution.py:113
  731.7 4.4 fusion.37
  736.1 71.6 %all-reduce.11.cloned.1.call-done = f32[2,1,20,2048]{3,0,2,1:T(2,128)} async-done(((f32[2,1,20,2048]{3,0,2,1:T(2,128)}), f32[2,1,20,2048]{3,0,2,1:T(2,128)}) %all-reduce.11.cloned.1.call-update) | async-done | bytes 327696 | tf_op jit(solution)/shard_map/psum | solution.py:113
  810.1 321.5 %all-gather.1 = f32[256,1,20,16]{2,3,1,0:T(8,128)S(1)} all-gather(f32[2,1,20,16]{2,3,1,0:T(8,128)S(1)} %pad_maximum_fusion.9), channel_id=3, replica_groups=mesh['gx'=16,'gy'=8] {'gx','gy'}, dimensions={0}, use_global_device_ids=true | all-gather | bytes 330240 | tf_op jit(solution)/shard_map/all_gather | solution.py:128
  1135.8 2.2 convolution_bitcast_fusion.1
  1138.0 10.5 fusion.54
  (215 shorter events, 84.6 us)
Async XLA Ops:
  6.5 15.7 %copy-start.7 = (bf16[2,20,500]{2,0,1:T(2,128)(2,1)S(1)}, bf16[2,20,500]{2,0,1:T(2,128)(2,1)}, u32[]{:S(2)}) copy-start(bf16[2,20,500]{2,0,1:T(2,128)(2,1)} %param.9) | copy-start | bytes 120004
  6.5 150.1 %all-reduce.5.cloned.1.call-start = ((), (), s32[]{:S(2)}) async-start(), calls=%async_computation | async-start | bytes 655360 | tf_op jit(solution)/shard_map/psum | solution.py:113
  8.1 19.1 %collective-permute-start = (bf16[1,20,4,256]{3,1,2,0:T(8,128)(2,1)}, bf16[1,20,4,256]{3,1,2,0:T(8,128)(2,1)S(1)}, u32[]{:S(2)}, u32[]{:S(2)}) collective-permute-start(bf16[1,20,4,256]{3,1,2,0:T(8,128)(2,1)} %copy.500), channel_id=1, source_target_pairs={{0,8},{8,16},{16,24},{24,32},{32,40},{40,48},{48,56},{56,64},{64,7... | collective-permute-start | bytes 122888 | tf_op jit(solution)/shard_map/ppermute | solution.py:25
  8.8 19.2 %collective-permute-start.1 = (bf16[1,20,4,256]{3,1,2,0:T(8,128)(2,1)}, bf16[1,20,4,256]{3,1,2,0:T(8,128)(2,1)S(1)}, u32[]{:S(2)}, u32[]{:S(2)}) collective-permute-start(bf16[1,20,4,256]{3,1,2,0:T(8,128)(2,1)} %copy.501), channel_id=1, source_target_pairs={{8,0},{16,8},{24,16},{32,24},{40,32},{48,40},{56,48},{64,56},{72,6... | collective-permute-start | bytes 122888 | tf_op jit(solution)/shard_map/ppermute | solution.py:26
  15.0 7.2 copy-start.11
  15.0 7.2 copy-start.13
  15.0 10.1 copy-start.20
  15.0 10.8 copy-start.21
  15.0 12.1 %copy-start.10 = (bf16[2,20,180]{2,0,1:T(2,128)(2,1)S(1)}, bf16[2,20,180]{2,0,1:T(2,128)(2,1)}, u32[]{:S(2)}) copy-start(bf16[2,20,180]{2,0,1:T(2,128)(2,1)} %param.8) | copy-start | bytes 43204
  15.0 12.2 %copy-start.1 = (bf16[1,20,128,256]{3,2,1,0:T(8,128)(2,1)S(1)}, bf16[1,20,128,256]{3,2,1,0:T(8,128)(2,1)}, u32[]{:S(2)}) copy-start(bf16[1,20,128,256]{3,2,1,0:T(8,128)(2,1)} %param.6) | copy-start | bytes 3932164
  22.1 210.8 %all-reduce.7.cloned.1.call-start = ((), (), s32[]{:S(2)}) async-start(), calls=%async_computation.1 | async-start | bytes 655360 | tf_op jit(solution)/shard_map/psum | solution.py:113
  28.0 1.2 copy-start
  30.2 9.5 collective-permute-start.2
  32.4 7.8 collective-permute-start.3
  65.8 3.8 copy-start.16
  95.1 4.3 copy-start.6
  101.7 8.9 slice-start
  101.7 8.9 slice-start.1
  104.2 6.5 slice-start.2
  110.6 2.4 copy-start.4
  156.7 575.0 %all-reduce.9.cloned.1.call-start = ((), (), s32[]{:S(2)}) async-start(), calls=%async_computation.2 | async-start | bytes 655360 | tf_op jit(solution)/shard_map/psum | solution.py:113
  161.2 407.2 %copy-start.5 = (f32[32,256]{1,0:T(8,128)S(1)}, f32[32,256]{1,0:T(8,128)}, u32[]{:S(2)}) copy-start(f32[32,256]{1,0:T(8,128)} %get-tuple-element.296) | copy-start | bytes 98308
  561.6 9.0 copy-start.2
  568.3 12.7 %copy-start.12 = (bf16[256,32]{0,1:T(8,128)(2,1)S(1)}, bf16[256,32]{0,1:T(8,128)(2,1)}, u32[]{:S(2)}) copy-start(bf16[256,32]{0,1:T(8,128)(2,1)} %copy-done.11) | copy-start | bytes 49156
  568.3 12.7 %copy-start.14 = (bf16[256,32]{0,1:T(8,128)(2,1)S(1)}, bf16[256,32]{0,1:T(8,128)(2,1)}, u32[]{:S(2)}) copy-start(bf16[256,32]{0,1:T(8,128)(2,1)} %copy-done.13) | copy-start | bytes 49156
  584.1 7.1 collective-permute-start.4
  584.2 7.0 collective-permute-start.5
  592.9 6.2 collective-permute-start.6
  595.6 4.1 collective-permute-start.7
  598.7 209.0 %all-reduce.11.cloned.1.call-start = ((), (), s32[]{:S(2)}) async-start(), calls=%async_computation.3 | async-start | bytes 655360 | tf_op jit(solution)/shard_map/psum | solution.py:113
  616.2 3.2 copy-start.19
  635.6 11.1 copy-start.8
  643.2 3.3 copy-start.17
  643.2 8.0 copy-start.15
  651.2 9.6 copy-start.18
  666.1 5.3 copy-start.9
  673.9 134.9 %copy-start.3 = (f32[20,20,16]{1,2,0:T(8,128)S(1)}, f32[20,20,16]{1,2,0:T(8,128)}, u32[]{:S(2)}) copy-start(f32[20,20,16]{1,2,0:T(8,128)} %get-tuple-element.285) | copy-start | bytes 76804
Sparse Core Ops, SparseCore 0:
  22.2 134.3 all-reduce.4
  159.3 73.6 all-reduce.6
  598.8 132.7 all-reduce.8
  734.1 73.5 all-reduce.10
